TPU v7x, 32 devices: a whole 2x2x4 slice. The times are simulated.
32 devices in a mesh: dp: 8 (over y, x, core), tensor: 4 (over z).
Axes of the slice: x: 2, y: 2, z: 4, core: 2. Of those that a mesh axis runs over, the one named last changes fastest.
Arguments:
- tokens_in: bfloat16 [4096, 1024], P(('dp', 'tensor')), may hold values from -6 to 6
- attn_gain: float32 [1024], replicated, may hold values from 0.1 to 1.9
- w_query: bfloat16 [1024, 2048], P(None, 'tensor'), may hold values from -0.1875 to 0.1875
- w_key: bfloat16 [1024, 1024], P(None, 'tensor'), may hold values from -0.1875 to 0.1875
- w_value: bfloat16 [1024, 1024], P(None, 'tensor'), may hold values from -0.1875 to 0.1875
- query_gain: float32 [128], replicated, may hold values from 0.5 to 2.5, as said below
- key_gain: float32 [128], replicated, may hold values from 0.5 to 2.5, as said below
- w_output: bfloat16 [2048, 1024], P('tensor'), may hold values from -0.5 to 0.5
- mlp_gain: float32 [1024], replicated, may hold values from 0.1 to 1.9
- w_gate: bfloat16 [1024, 3072], P(None, 'tensor'), may hold values from -0.1875 to 0.1875
- w_up: bfloat16 [1024, 3072], P(None, 'tensor'), may hold values from -0.1875 to 0.1875
- w_down: bfloat16 [3072, 1024], P('tensor'), may hold values from -0.109375 to 0.109375
- out_cotangent: bfloat16 [4096, 1024], P(('dp', 'tensor')), may hold values from -6 to 6
Outputs:
- block_out: bfloat16 [4096, 1024], P(('dp', 'tensor'))
- grad_input: bfloat16 [4096, 1024], P(('dp', 'tensor'))
- grad_attn_gain: float32 [1024], replicated
- grad_w_query: float32 [1024, 2048], P('dp', 'tensor')
- grad_w_key: float32 [1024, 1024], P('dp', 'tensor')
- grad_w_value: float32 [1024, 1024], P('dp', 'tensor')
- grad_query_gain: float32 [128], replicated
- grad_key_gain: float32 [128], replicated
- grad_w_output: float32 [2048, 1024], P('tensor', 'dp')
- grad_mlp_gain: float32 [1024], replicated
- grad_w_gate: float32 [1024, 3072], P('dp', 'tensor')
- grad_w_up: float32 [1024, 3072], P('dp', 'tensor')
- grad_w_down: float32 [3072, 1024], P('tensor', 'dp')
Inputs may be any that keep to these rules, and one draw needn't show every extreme that they name: `query_gain`: positive gains. `key_gain`: positive gains.
All inputs are finite; a program needn't handle non-finite values.
Results may differ from a plain program's by a relative error of at most 0.025.
Values may be sent and summed in bfloat16 or wider, within the bound.
A program may use at most 128 MiB of HBM per device.

v0:
```python
import jax
import jax.numpy as jnp
from jax import lax
from jax.sharding import PartitionSpec as P

SEQ = 512
EPS = 1e-06
THETA = 1000000.0


def rope_tables(length, head_width):
    half_width = head_width // 2
    inverse_freq = THETA ** (-(jnp.arange(half_width, dtype=jnp.float32) * 2.0 / head_width))
    positions = jnp.arange(length, dtype=jnp.float32)
    angles = positions[:, None] * inverse_freq[None, :]
    return (jnp.cos(angles)[:, None, :], jnp.sin(angles)[:, None, :])


def rope_apply(values, cosine_table, sine_table):
    half_width = values.shape[-1] // 2
    first_half = values[..., :half_width]
    second_half = values[..., half_width:]
    return jnp.concatenate(
        [
            first_half * cosine_table - second_half * sine_table,
            second_half * cosine_table + first_half * sine_table,
        ],
        axis=-1,
    )


def rope_back(grad_rows, cosine_table, sine_table):
    half_width = grad_rows.shape[-1] // 2
    first_half = grad_rows[..., :half_width]
    second_half = grad_rows[..., half_width:]
    return jnp.concatenate(
        [
            first_half * cosine_table + second_half * sine_table,
            second_half * cosine_table - first_half * sine_table,
        ],
        axis=-1,
    )


def row_scale(values):
    return lax.rsqrt(jnp.mean(values * values, axis=-1, keepdims=True) + EPS)


def norm_back(grad_out, values, scale_rows, gain_row):
    weighted = grad_out * gain_row
    inner_mean = jnp.mean(weighted * values, axis=-1, keepdims=True)
    return scale_rows * weighted - values * scale_rows**3 * inner_mean


def own_rows(values, start, count):
    return lax.dynamic_slice_in_dim(values, start, count, 0)


def causal_scores(grouped, key_seq, factor):
    length = grouped.shape[0]
    scores = (
        jnp.einsum("qgrd,kgd->grqk", grouped, key_seq, preferred_element_type=jnp.float32) * factor
    )
    rows_at = lax.broadcasted_iota(jnp.int32, (length, length), 0)
    cols_at = lax.broadcasted_iota(jnp.int32, (length, length), 1)
    return jnp.where(cols_at <= rows_at, scores, -jnp.inf)


def attend_forward(inputs):
    query_seq, key_seq, value_seq = inputs
    length, head_count, head_width = query_seq.shape
    kv_count = key_seq.shape[1]
    grouped = query_seq.reshape(length, kv_count, head_count // kv_count, head_width)
    scores = causal_scores(grouped, key_seq, head_width ** (-0.5))
    top_score = jnp.max(scores, axis=-1, keepdims=True)
    log_total = top_score + jnp.log(jnp.sum(jnp.exp(scores - top_score), axis=-1, keepdims=True))
    prob_low = jnp.exp(scores - log_total).astype(jnp.bfloat16)
    mixed_seq = jnp.einsum(
        "grqk,kgd->qgrd", prob_low, value_seq, preferred_element_type=jnp.float32
    )
    return (mixed_seq.astype(jnp.bfloat16).reshape(length, head_count, head_width), log_total)


def attend_backward(inputs):
    query_seq, key_seq, value_seq, mixed_seq, log_total, grad_mixed = inputs
    length, head_count, head_width = query_seq.shape
    kv_count = key_seq.shape[1]
    ratio = head_count // kv_count
    factor = head_width ** (-0.5)
    grouped = query_seq.reshape(length, kv_count, ratio, head_width)
    scores = causal_scores(grouped, key_seq, factor)
    prob_full = jnp.exp(scores - log_total)
    prob_low = prob_full.astype(jnp.bfloat16)
    grad_grouped = grad_mixed.reshape(length, kv_count, ratio, head_width)
    inner_rows = jnp.sum(grad_mixed.astype(jnp.float32) * mixed_seq.astype(jnp.float32), axis=-1)
    inner_rows = jnp.transpose(inner_rows.reshape(length, kv_count, ratio), (1, 2, 0))[..., None]
    grad_probs = jnp.einsum(
        "qgrd,kgd->grqk", grad_grouped, value_seq, preferred_element_type=jnp.float32
    )
    grad_scores = (prob_full * (grad_probs - inner_rows)).astype(jnp.bfloat16)
    grad_query = (
        jnp.einsum("grqk,kgd->qgrd", grad_scores, key_seq, preferred_element_type=jnp.float32)
        * factor
    )
    grad_key = (
        jnp.einsum("grqk,qgrd->kgd", grad_scores, grouped, preferred_element_type=jnp.float32)
        * factor
    )
    grad_value = jnp.einsum(
        "grqk,qgrd->kgd", prob_low, grad_grouped, preferred_element_type=jnp.float32
    )
    return (grad_query.reshape(length, head_count, head_width), grad_key, grad_value)


def on_device(
    tokens_in,
    attn_gain,
    w_query,
    w_key,
    w_value,
    query_gain,
    key_gain,
    w_output,
    mlp_gain,
    w_gate,
    w_up,
    w_down,
    out_cotangent,
):
    row_share = tokens_in.shape[0]
    row_start = lax.axis_index("tensor") * row_share
    head_width = query_gain.shape[0]
    head_count = w_query.shape[1] // head_width
    kv_count = w_key.shape[1] // head_width
    cosine_table, sine_table = rope_tables(SEQ, head_width)
    resid_in = lax.all_gather(tokens_in, "tensor", axis=0, tiled=True).astype(jnp.float32)
    scale_one = row_scale(resid_in)
    normed_one = (resid_in * scale_one * attn_gain).astype(jnp.bfloat16)
    tok_count = normed_one.shape[0]
    seq_count = tok_count // SEQ
    query_lin = jnp.dot(normed_one, w_query, preferred_element_type=jnp.float32).reshape(
        tok_count, head_count, head_width
    )
    key_lin = jnp.dot(normed_one, w_key, preferred_element_type=jnp.float32).reshape(
        tok_count, kv_count, head_width
    )
    value_heads = (
        jnp.dot(normed_one, w_value, preferred_element_type=jnp.float32)
        .astype(jnp.bfloat16)
        .reshape(seq_count, SEQ, kv_count, head_width)
    )
    query_scale = row_scale(query_lin)
    key_scale = row_scale(key_lin)
    query_rot = rope_apply(
        (query_lin * query_scale * query_gain).reshape(seq_count, SEQ, head_count, head_width),
        cosine_table,
        sine_table,
    ).astype(jnp.bfloat16)
    key_rot = rope_apply(
        (key_lin * key_scale * key_gain).reshape(seq_count, SEQ, kv_count, head_width),
        cosine_table,
        sine_table,
    ).astype(jnp.bfloat16)
    mixed_heads, log_totals = lax.map(attend_forward, (query_rot, key_rot, value_heads))
    attn_flat = mixed_heads.reshape(tok_count, head_count * head_width)
    attn_part = jnp.dot(attn_flat, w_output, preferred_element_type=jnp.float32)
    hidden = resid_in + lax.psum(attn_part.astype(jnp.bfloat16), "tensor").astype(jnp.float32)
    scale_two = row_scale(hidden)
    normed_two = (hidden * scale_two * mlp_gain).astype(jnp.bfloat16)
    gate_lin = jnp.dot(normed_two, w_gate, preferred_element_type=jnp.float32)
    up_lin = jnp.dot(normed_two, w_up, preferred_element_type=jnp.float32)
    gate_sig = jax.nn.sigmoid(gate_lin)
    activated = (gate_lin * gate_sig * up_lin).astype(jnp.bfloat16)
    mlp_part = jnp.dot(activated, w_down, preferred_element_type=jnp.float32)
    output_all = hidden + lax.psum(mlp_part.astype(jnp.bfloat16), "tensor").astype(jnp.float32)
    block_out = own_rows(output_all, row_start, row_share).astype(jnp.bfloat16)
    grad_all = lax.all_gather(out_cotangent, "tensor", axis=0, tiled=True)
    grad_down = jnp.dot(activated.T, grad_all, preferred_element_type=jnp.float32)
    grad_act = jnp.dot(grad_all, w_down.T, preferred_element_type=jnp.float32)
    grad_gate = (grad_act * up_lin * gate_sig * (1.0 + gate_lin * (1.0 - gate_sig))).astype(
        jnp.bfloat16
    )
    grad_up = (grad_act * gate_lin * gate_sig).astype(jnp.bfloat16)
    grad_w_gate = jnp.dot(normed_two.T, grad_gate, preferred_element_type=jnp.float32)
    grad_w_up = jnp.dot(normed_two.T, grad_up, preferred_element_type=jnp.float32)
    back_two = jnp.dot(grad_gate, w_gate.T, preferred_element_type=jnp.float32) + jnp.dot(
        grad_up, w_up.T, preferred_element_type=jnp.float32
    )
    grad_norm_two = lax.psum(back_two, "tensor")
    grad_hidden = grad_all.astype(jnp.float32) + norm_back(
        grad_norm_two, hidden, scale_two, mlp_gain
    )
    gain_two = jnp.sum(
        own_rows(grad_norm_two, row_start, row_share)
        * own_rows(hidden * scale_two, row_start, row_share),
        axis=0,
    )
    grad_hidden_low = grad_hidden.astype(jnp.bfloat16)
    grad_w_output = jnp.dot(attn_flat.T, grad_hidden_low, preferred_element_type=jnp.float32)
    grad_mixed = (
        jnp.dot(grad_hidden_low, w_output.T, preferred_element_type=jnp.float32)
        .astype(jnp.bfloat16)
        .reshape(seq_count, SEQ, head_count, head_width)
    )
    grad_query_rot, grad_key_rot, grad_values = lax.map(
        attend_backward, (query_rot, key_rot, value_heads, mixed_heads, log_totals, grad_mixed)
    )
    grad_query_pre = rope_back(grad_query_rot, cosine_table, sine_table).reshape(
        tok_count, head_count, head_width
    )
    grad_key_pre = rope_back(grad_key_rot, cosine_table, sine_table).reshape(
        tok_count, kv_count, head_width
    )
    gain_query = jnp.sum(grad_query_pre * query_lin * query_scale, axis=(0, 1))
    gain_key = jnp.sum(grad_key_pre * key_lin * key_scale, axis=(0, 1))
    grad_query_low = (
        norm_back(grad_query_pre, query_lin, query_scale, query_gain)
        .astype(jnp.bfloat16)
        .reshape(tok_count, head_count * head_width)
    )
    grad_key_low = (
        norm_back(grad_key_pre, key_lin, key_scale, key_gain)
        .astype(jnp.bfloat16)
        .reshape(tok_count, kv_count * head_width)
    )
    grad_value_low = grad_values.astype(jnp.bfloat16).reshape(tok_count, kv_count * head_width)
    grad_w_query = jnp.dot(normed_one.T, grad_query_low, preferred_element_type=jnp.float32)
    grad_w_key = jnp.dot(normed_one.T, grad_key_low, preferred_element_type=jnp.float32)
    grad_w_value = jnp.dot(normed_one.T, grad_value_low, preferred_element_type=jnp.float32)
    back_one = (
        jnp.dot(grad_query_low, w_query.T, preferred_element_type=jnp.float32)
        + jnp.dot(grad_key_low, w_key.T, preferred_element_type=jnp.float32)
        + jnp.dot(grad_value_low, w_value.T, preferred_element_type=jnp.float32)
    )
    grad_norm_one = lax.psum(back_one, "tensor")
    grad_input_all = grad_hidden + norm_back(grad_norm_one, resid_in, scale_one, attn_gain)
    grad_input = own_rows(grad_input_all, row_start, row_share).astype(jnp.bfloat16)
    gain_one = jnp.sum(
        own_rows(grad_norm_one, row_start, row_share)
        * own_rows(resid_in * scale_one, row_start, row_share),
        axis=0,
    )
    gain_one, gain_two, gain_query, gain_key = lax.psum(
        (gain_one, gain_two, gain_query, gain_key), ("dp", "tensor")
    )
    grad_w_query, grad_w_key, grad_w_value, grad_w_output, grad_w_gate, grad_w_up, grad_down = (
        lax.psum_scatter(grad_w_query, "dp", scatter_dimension=0, tiled=True),
        lax.psum_scatter(grad_w_key, "dp", scatter_dimension=0, tiled=True),
        lax.psum_scatter(grad_w_value, "dp", scatter_dimension=0, tiled=True),
        lax.psum_scatter(grad_w_output, "dp", scatter_dimension=1, tiled=True),
        lax.psum_scatter(grad_w_gate, "dp", scatter_dimension=0, tiled=True),
        lax.psum_scatter(grad_w_up, "dp", scatter_dimension=0, tiled=True),
        lax.psum_scatter(grad_down, "dp", scatter_dimension=1, tiled=True),
    )
    return (
        block_out,
        grad_input,
        gain_one,
        grad_w_query,
        grad_w_key,
        grad_w_value,
        gain_query,
        gain_key,
        grad_w_output,
        gain_two,
        grad_w_gate,
        grad_w_up,
        grad_down,
    )


def solution(mesh):
    in_specs = (
        P(("dp", "tensor"), None),
        P(),
        P(None, "tensor"),
        P(None, "tensor"),
        P(None, "tensor"),
        P(),
        P(),
        P("tensor", None),
        P(),
        P(None, "tensor"),
        P(None, "tensor"),
        P("tensor", None),
        P(("dp", "tensor"), None),
    )
    out_specs = (
        P(("dp", "tensor"), None),
        P(("dp", "tensor"), None),
        P(),
        P("dp", "tensor"),
        P("dp", "tensor"),
        P("dp", "tensor"),
        P(),
        P(),
        P("tensor", "dp"),
        P(),
        P("dp", "tensor"),
        P("dp", "tensor"),
        P("tensor", "dp"),
    )
    return jax.shard_map(
        on_device, mesh=mesh, in_specs=in_specs, out_specs=out_specs, check_vma=False
    )
```

profile of v0, /device:TPU:0, one launch (start us, length us, event | category | flops | bytes accessed | tf_op | source)
XLA Modules:
  0.0 707.4 jit_solution(18238567241741866970)
XLA Ops:
  9.3 31.0 %all-gather.3.cloned.1.call-done = bf16[512,1024]{1,0:T(8,128)(2,1)} async-done(((bf16[128,1024]{1,0:T(8,128)(2,1)}), bf16[512,1024]{1,0:T(8,128)(2,1)}) %all-gather.3.cloned.1.call-update) | async-done | bytes 1048592 | tf_op jit(solution)/shard_map/all_gather | solution.py:136
  40.3 1.5 multiply_reduce_fusion.3
  42.4 2.4 multiply_reduce_fusion.4
  48.2 2.0 copy.29
  50.2 3.0 multiply_reduce_fusion.7
  53.3 2.0 copy.26
  55.3 1.3 multiply_multiply_fusion.3
  59.2 1.3 fusion.3
  62.6 1.4 convolution_convert_fusion.2
  64.8 1.7 convolution_convert_fusion.1
  67.5 50.4 %all-reduce.6.cloned.1.call-done = bf16[512,1024]{1,0:T(8,128)(2,1)} async-done(((bf16[512,1024]{1,0:T(8,128)(2,1)}), bf16[512,1024]{1,0:T(8,128)(2,1)}) %all-reduce.6.cloned.1.call-update) | async-done | bytes 1048592 | tf_op jit(solution)/shard_map/psum | solution.py:167
  117.9 3.1 convert_multiply_fusion
  121.7 1.8 multiply_convert_fusion
  123.4 2.1 fusion.44
  125.6 2.1 fusion.45
  127.7 19.1 %all-gather.5.cloned.1.call-done = bf16[512,1024]{1,0:T(8,128)(2,1)} async-done(((bf16[128,1024]{1,0:T(8,128)(2,1)}), bf16[512,1024]{1,0:T(8,128)(2,1)}) %all-gather.5.cloned.1.call-update) | async-done | bytes 1048592 | tf_op jit(solution)/shard_map/all_gather | solution.py:177
  146.8 4.7 multiply_convert_fusion.2
  153.5 2.4 convolution_add_fusion
  158.5 2.1 copy.41
  160.5 3.2 convolution_convert_fusion
  164.0 77.6 %all-reduce.10.cloned.1.call-done = f32[512,1024]{1,0:T(8,128)} async-done(((f32[512,1024]{1,0:T(8,128)}), f32[512,1024]{1,0:T(8,128)}) %all-reduce.10.cloned.1.call-update) | async-done | bytes 2097168 | tf_op jit(solution)/shard_map/psum | solution.py:189
  241.6 2.5 multiply_reduce_fusion.1
  244.4 2.9 subtract_add_fusion
  249.4 3.7 fusion.1
  257.9 2.1 fusion.47
  262.0 1.7 fusion.48
  264.2 2.5 fusion.6
  266.8 1.8 add_add_fusion
  269.3 1.6 fusion.40
  271.0 1.6 fusion.39
  272.7 3.8 fusion.49
  276.8 3.8 fusion.50
  281.9 3.8 fusion.51
  285.8 2.3 fusion.41
  288.2 3.6 fusion.26
  292.7 1.6 convert_element_type.102
  294.3 1.3 multiply_reduce_fusion.5
  295.6 1.9 fusion.18
  297.5 85.0 %all-reduce.12.cloned.1.call-done = f32[512,1024]{1,0:T(8,128)} async-done(((f32[512,1024]{1,0:T(8,128)}), f32[512,1024]{1,0:T(8,128)}) %all-reduce.12.cloned.1.call-update) | async-done | bytes 2097168 | tf_op jit(solution)/shard_map/psum | solution.py:235
  382.4 3.3 multiply_reduce_fusion
  387.1 39.4 %all-reduce = (f32[1024]{0:T(1024)}, f32[128]{0:T(128)}, f32[128]{0:T(128)}, f32[1024]{0:T(1024)}) all-reduce(f32[1024]{0:T(1024)S(1)} %multiply_reduce_fusion.6, f32[128]{0:T(128)S(1)} %get-tuple-element.53, f32[128]{0:T(128)S(1)} %get-tuple-element.51, ...), channel_id=1, replica_groups=mesh['dp'=8,'tensor'=4] {'dp','tensor'}, use_global_device_ids=true, to_apply=%region_16.17 | all-reduce | flops 2304 | bytes 18432 | tf_op jit(solution)/shard_map/psum | solution.py:243
  426.5 2.2 fusion.15
  428.8 32.3 %reduce-scatter.12.cloned.1.call-done = f32[128,256]{1,0:T(8,128)} async-done(((f32[1024,256]{1,0:T(8,128)}), f32[128,256]{1,0:T(8,128)}) %reduce-scatter.12.cloned.1.call-update) | async-done | bytes 131088 | tf_op jit(solution)/shard_map/reduce_scatter | solution.py:249
  461.0 50.0 %reduce-scatter.16.cloned.1.call-done = f32[128,768]{1,0:T(8,128)} async-done(((f32[1024,768]{1,0:T(8,128)}), f32[128,768]{1,0:T(8,128)}) %reduce-scatter.16.cloned.1.call-update) | async-done | bytes 393232 | tf_op jit(solution)/shard_map/reduce_scatter | solution.py:251
  511.1 49.9 %reduce-scatter.18.cloned.1.call-done = f32[128,768]{1,0:T(8,128)} async-done(((f32[1024,768]{1,0:T(8,128)}), f32[128,768]{1,0:T(8,128)}) %reduce-scatter.18.cloned.1.call-update) | async-done | bytes 393232 | tf_op jit(solution)/shard_map/reduce_scatter | solution.py:252
  561.0 50.0 %reduce-scatter.20.cloned.1.call-done = f32[768,128]{1,0:T(8,128)} async-done(((f32[768,1024]{1,0:T(8,128)}), f32[768,128]{1,0:T(8,128)}) %reduce-scatter.20.cloned.1.call-update) | async-done | bytes 393232 | tf_op jit(solution)/shard_map/reduce_scatter | solution.py:253
  611.0 44.8 %reduce-scatter.8.cloned.1.call-done = f32[128,512]{1,0:T(8,128)} async-done(((f32[1024,512]{1,0:T(8,128)}), f32[128,512]{1,0:T(8,128)}) %reduce-scatter.8.cloned.1.call-update) | async-done | bytes 262160 | tf_op jit(solution)/shard_map/reduce_scatter | solution.py:247
  655.9 45.0 %reduce-scatter.14.cloned.1.call-done = f32[512,128]{1,0:T(8,128)} async-done(((f32[512,1024]{1,0:T(8,128)}), f32[512,128]{1,0:T(8,128)}) %reduce-scatter.14.cloned.1.call-update) | async-done | bytes 262160 | tf_op jit(solution)/shard_map/reduce_scatter | solution.py:250
  (191 shorter events, 31.8 us)
Async XLA Ops:
  7.2 139.6 %copy-start = (bf16[768,1024]{1,0:T(8,128)(2,1)S(1)}, bf16[768,1024]{1,0:T(8,128)(2,1)}, u32[]{:S(2)}) copy-start(bf16[768,1024]{1,0:T(8,128)(2,1)} %param.24) | copy-start | bytes 4718596
  7.2 35.2 %copy-start.49 = (f32[1024]{0:T(1024)S(1)}, f32[1024]{0:T(1024)}, u32[]{:S(2)}) copy-start(f32[1024]{0:T(1024)} %param.14) | copy-start | bytes 12292
  7.2 33.1 %all-gather.3.cloned.1.call-start = ((), (), s32[]{:S(2)}) async-start(), calls=%async_computation.7 | async-start | bytes 1310720 | tf_op jit(solution)/shard_map/all_gather | solution.py:136
  7.9 110.0 %all-reduce.6.cloned.1.call-start = ((), (), s32[]{:S(2)}) async-start(), calls=%async_computation.8 | async-start | bytes 2097152 | tf_op jit(solution)/shard_map/psum | solution.py:167
  9.0 33.4 %copy-start.19 = (f32[512,64]{1,0:T(8,128)}, f32[512,64]{1,0:T(8,128)S(1)}, u32[]{:S(2)}) copy-start(f32[512,64]{1,0:T(8,128)S(1)} %get-tuple-element.97) | copy-start | bytes 393220
  9.0 33.4 %copy-start.21 = (f32[512,64]{1,0:T(8,128)}, f32[512,64]{1,0:T(8,128)S(1)}, u32[]{:S(2)}) copy-start(f32[512,64]{1,0:T(8,128)S(1)} %get-tuple-element.98) | copy-start | bytes 393220
  9.2 36.8 %copy-start.34 = (f32[512,64]{0,1:T(8,128)}, f32[512,64]{0,1:T(8,128)S(1)}, u32[]{:S(2)}) copy-start(f32[512,64]{0,1:T(8,128)S(1)} %copy.27) | copy-start | bytes 393220
  42.4 19.0 %copy-start.45 = (f32[512]{0:T(512)}, f32[512]{0:T(512)S(1)}, u32[]{:S(2)}) copy-start(f32[512]{0:T(512)S(1)} %get-tuple-element.94) | copy-start | bytes 6148
  42.4 3.4 copy-start.55
  46.0 4.2 copy-start.2
  55.3 3.9 copy-start.14
  60.5 2.1 copy-start.10
  61.9 2.0 copy-start.52
  62.6 2.2 copy-start.37
  66.5 80.3 %all-gather.5.cloned.1.call-start = ((), (), s32[]{:S(2)}) async-start(), calls=%async_computation.10 | async-start | bytes 1310720 | tf_op jit(solution)/shard_map/all_gather | solution.py:177
  67.3 54.4 %copy-start.43 = (f32[1024]{0:T(1024)S(1)}, f32[1024]{0:T(1024)}, u32[]{:S(2)}) copy-start(f32[1024]{0:T(1024)} %param.21) | copy-start | bytes 12292
  67.3 174.3 %all-reduce.10.cloned.1.call-start = ((), (), s32[]{:S(2)}) async-start(), calls=%async_computation.11 | async-start | bytes 4194304 | tf_op jit(solution)/shard_map/psum | solution.py:189
  117.9 3.7 copy-start.6
  121.6 1.8 copy-start.47
  121.6 1.8 copy-start.59
  123.4 2.2 copy-start.4
  123.4 2.2 copy-start.32
  146.8 4.7 copy-start.60
  151.5 2.0 copy-start.33
  155.9 139.7 %all-reduce.8.cloned.1.call-start = ((), (), s32[]{:S(2)}) async-start(), calls=%async_computation.9 | async-start | bytes 2097152 | tf_op jit(solution)/shard_map/psum | solution.py:175
  163.7 80.4 %copy-start.7 = (bf16[512,1024]{1,0:T(8,128)(2,1)S(1)}, bf16[512,1024]{1,0:T(8,128)(2,1)}, u32[]{:S(2)}) copy-start(bf16[512,1024]{1,0:T(8,128)(2,1)} %all-reduce.6.cloned.1.call-done) | copy-start | bytes 3145732
  163.7 218.7 %all-reduce.12.cloned.1.call-start = ((), (), s32[]{:S(2)}) async-start(), calls=%async_computation.12 | async-start | bytes 4194304 | tf_op jit(solution)/shard_map/psum | solution.py:235
  241.6 2.5 copy-start.12
  241.6 2.8 copy-start.17
  244.4 2.9 copy-start.30
  244.4 2.9 copy-start.38
  249.4 3.7 copy-start.25
  249.4 3.7 copy-start.27
  257.9 2.1 copy-start.20
  257.9 2.1 copy-start.22
  261.9 2.4 copy-start.11
  261.9 2.4 copy-start.53
  264.2 2.5 copy-start.13
  264.2 2.5 copy-start.41
  268.6 160.2 %reduce-scatter.10.cloned.1.call-start = ((), (), s32[]{:S(2)}) async-start(), calls=%async_computation.14 | async-start | bytes 1179648 | tf_op jit(solution)/shard_map/reduce_scatter | solution.py:248
  271.0 190.1 %reduce-scatter.12.cloned.1.call-start = ((), (), s32[]{:S(2)}) async-start(), calls=%async_computation.15 | async-start | bytes 1179648 | tf_op jit(solution)/shard_map/reduce_scatter | solution.py:249
  272.6 238.4 %reduce-scatter.16.cloned.1.call-start = ((), (), s32[]{:S(2)}) async-start(), calls=%async_computation.17 | async-start | bytes 3538944 | tf_op jit(solution)/shard_map/reduce_scatter | solution.py:251
  276.5 284.5 %reduce-scatter.18.cloned.1.call-start = ((), (), s32[]{:S(2)}) async-start(), calls=%async_computation.18 | async-start | bytes 3538944 | tf_op jit(solution)/shard_map/reduce_scatter | solution.py:252
  280.7 330.3 %reduce-scatter.20.cloned.1.call-start = ((), (), s32[]{:S(2)}) async-start(), calls=%async_computation.19 | async-start | bytes 3538944 | tf_op jit(solution)/shard_map/reduce_scatter | solution.py:253
  285.8 2.4 copy-start.31
  285.8 370.1 %reduce-scatter.8.cloned.1.call-start = ((), (), s32[]{:S(2)}) async-start(), calls=%async_computation.13 | async-start | bytes 2359296 | tf_op jit(solution)/shard_map/reduce_scatter | solution.py:247
  288.2 412.7 %reduce-scatter.14.cloned.1.call-start = ((), (), s32[]{:S(2)}) async-start(), calls=%async_computation.16 | async-start | bytes 2359296 | tf_op jit(solution)/shard_map/reduce_scatter | solution.py:250
  382.4 318.4 %copy-start.1 = (bf16[768,1024]{1,0:T(8,128)(2,1)S(1)}, bf16[768,1024]{1,0:T(8,128)(2,1)}, u32[]{:S(2)}) copy-start(bf16[768,1024]{1,0:T(8,128)(2,1)} %param.24) | copy-start | bytes 4718596
  (27 other events, 32.2 us)
Sparse Core Ops, SparseCore 0:
  9.6 30.6 all-gather.2
  66.7 51.2 all-reduce.5
  119.5 27.2 all-gather.4
  156.1 85.5 all-reduce.9
  243.8 50.9 all-reduce.7
  297.0 85.3 all-reduce.11
  386.2 34.9 reduce-scatter.9
  425.0 36.0 reduce-scatter.11
  465.0 46.0 reduce-scatter.15
  514.9 46.0 reduce-scatter.17
  564.9 46.0 reduce-scatter.19
  614.7 41.0 reduce-scatter.7
  659.7 41.1 reduce-scatter.13
where the time goes:
time: 709 us; the launch traced here: 707 us
  waiting for transfers between devices  537 us (76%)
  matrix products  60.7 us (9%)
  blocking collectives  39.4 us (6%)
  other arithmetic  33.8 us (5%)
  local copies, waits for them, and re-layouts  20.9 us (3%)
  between operations  14.6 us (2%)
    psum x1, waiting for transfers between devices, on_device(): grad_norm_one = lax.psum(back_one, 'tensor')  85 us
    psum x1, waiting for transfers between devices, on_device(): grad_norm_two = lax.psum(back_two, 'tensor')  77.6 us
    psum x1, waiting for transfers between devices, on_device(): lax.psum(attn_part.astype(jnp.bfloat16), 'tensor').astype(jnp.float32)  50.4 us
    reduce_scatter x1, waiting for transfers between devices, on_device(): lax.psum_scatter(grad_w_gate, 'dp', scatter_dimension=0, tiled=True)  50 us
    reduce_scatter x1, waiting for transfers between devices, on_device(): lax.psum_scatter(grad_down, 'dp', scatter_dimension=1, tiled=True)  50 us
    reduce_scatter x1, waiting for transfers between devices, on_device(): lax.psum_scatter(grad_w_up, 'dp', scatter_dimension=0, tiled=True)  49.9 us
    reduce_scatter x1, waiting for transfers between devices, on_device(): lax.psum_scatter(grad_w_output, 'dp', scatter_dimension=1, tiled=True)  45 us
    reduce_scatter x1, waiting for transfers between devices, on_device(): lax.psum_scatter(grad_w_query, 'dp', scatter_dimension=0, tiled=True)  44.8 us
  transfers between devices with their start and end apart: 13, of which 11 were waited for; matrix products, arithmetic and copies ran while one was open for 10% of the time, Pallas kernels for 0%

commit v1 on v0

--- a/solution.py
+++ b/solution.py
@@ -232,7 +232,8 @@
         + jnp.dot(grad_key_low, w_key.T, preferred_element_type=jnp.float32)
         + jnp.dot(grad_value_low, w_value.T, preferred_element_type=jnp.float32)
     )
-    grad_norm_one = lax.psum(back_one, "tensor")
+    parts = lax.all_gather(back_one, "tensor", axis=0, tiled=False)
+    grad_norm_one = parts.sum(axis=0)
     grad_input_all = grad_hidden + norm_back(grad_norm_one, resid_in, scale_one, attn_gain)
     grad_input = own_rows(grad_input_all, row_start, row_share).astype(jnp.bfloat16)
     gain_one = jnp.sum(

time: 709 us -> 770 us (1.086)
  waiting for transfers between devices: 537 us -> 594 us
    all_gather x0 -> x1, waiting for transfers between devices: none -> 148 us  [on_device(): parts = lax.all_gather(back_one, 'tensor', axis=0, tiled=False)]
    psum x1 -> x0, waiting for transfers between devices: 85 us -> none  [on_device(): grad_norm_one = lax.psum(back_one, 'tensor')]
where the time goes in v1:
time: 770 us; the launch traced here: 769 us
  waiting for transfers between devices  594 us (77%)
  matrix products  60.6 us (8%)
  other arithmetic  39.7 us (5%)
  blocking collectives  38.6 us (5%)
  local copies, waits for them, and re-layouts  21 us (3%)
  between operations  14.6 us (2%)
    all_gather x1, waiting for transfers between devices, on_device(): parts = lax.all_gather(back_one, 'tensor', axis=0, tiled=False)  148 us
    psum x1, waiting for transfers between devices, on_device(): grad_norm_two = lax.psum(back_two, 'tensor')  77.6 us
    psum x1, waiting for transfers between devices, on_device(): lax.psum(attn_part.astype(jnp.bfloat16), 'tensor').astype(jnp.float32)  50.4 us
    reduce_scatter x1, waiting for transfers between devices, on_device(): lax.psum_scatter(grad_w_gate, 'dp', scatter_dimension=0, tiled=True)  50 us
    reduce_scatter x1, waiting for transfers between devices, on_device(): lax.psum_scatter(grad_down, 'dp', scatter_dimension=1, tiled=True)  50 us
    reduce_scatter x1, waiting for transfers between devices, on_device(): lax.psum_scatter(grad_w_up, 'dp', scatter_dimension=0, tiled=True)  49.9 us
    reduce_scatter x1, waiting for transfers between devices, on_device(): lax.psum_scatter(grad_w_output, 'dp', scatter_dimension=1, tiled=True)  45 us
    reduce_scatter x1, waiting for transfers between devices, on_device(): lax.psum_scatter(grad_w_query, 'dp', scatter_dimension=0, tiled=True)  44.9 us
  transfers between devices with their start and end apart: 13, of which 11 were waited for; matrix products, arithmetic and copies ran while one was open for 10% of the time, Pallas kernels for 0%

profile of v1, /device:TPU:0, one launch (start us, length us, event | category | flops | bytes accessed | tf_op | source)
XLA Modules:
  0.0 769.3 jit_solution(6335201233380734782)
XLA Ops:
  9.3 31.0 %all-gather.5.cloned.1.call-done = bf16[512,1024]{1,0:T(8,128)(2,1)} async-done(((bf16[128,1024]{1,0:T(8,128)(2,1)}), bf16[512,1024]{1,0:T(8,128)(2,1)}) %all-gather.5.cloned.1.call-update) | async-done | bytes 1048592 | tf_op jit(solution)/shard_map/all_gather | solution.py:136
  40.3 1.5 multiply_reduce_fusion.3
  42.4 2.4 multiply_reduce_fusion.4
  48.2 2.0 copy.29
  50.2 3.1 multiply_reduce_fusion.7
  53.3 2.0 copy.26
  55.4 1.3 multiply_multiply_fusion.3
  62.6 1.4 convolution_convert_fusion.2
  64.8 1.7 convolution_convert_fusion.1
  67.6 50.4 %all-reduce.5.cloned.1.call-done = bf16[512,1024]{1,0:T(8,128)(2,1)} async-done(((bf16[512,1024]{1,0:T(8,128)(2,1)}), bf16[512,1024]{1,0:T(8,128)(2,1)}) %all-reduce.5.cloned.1.call-update) | async-done | bytes 1048592 | tf_op jit(solution)/shard_map/psum | solution.py:167
  118.0 3.1 convert_multiply_fusion
  121.7 1.7 multiply_convert_fusion
  123.5 2.1 fusion.44
  125.6 2.1 fusion.45
  127.8 19.1 %all-gather.7.cloned.1.call-done = bf16[512,1024]{1,0:T(8,128)(2,1)} async-done(((bf16[128,1024]{1,0:T(8,128)(2,1)}), bf16[512,1024]{1,0:T(8,128)(2,1)}) %all-gather.7.cloned.1.call-update) | async-done | bytes 1048592 | tf_op jit(solution)/shard_map/all_gather | solution.py:177
  146.9 4.7 multiply_convert_fusion.2
  153.6 2.4 convolution_add_fusion
  158.5 2.0 copy.41
  160.5 3.2 convolution_convert_fusion
  164.0 77.6 %all-reduce.9.cloned.1.call-done = f32[512,1024]{1,0:T(8,128)} async-done(((f32[512,1024]{1,0:T(8,128)}), f32[512,1024]{1,0:T(8,128)}) %all-reduce.9.cloned.1.call-update) | async-done | bytes 2097168 | tf_op jit(solution)/shard_map/psum | solution.py:189
  241.7 2.5 multiply_reduce_fusion.1
  244.5 2.8 subtract_add_fusion
  249.5 3.7 fusion.1
  258.0 2.1 fusion.47
  262.1 1.7 fusion.48
  264.3 2.5 fusion.6
  266.8 1.8 add_add_fusion
  269.3 1.6 fusion.40
  271.0 1.6 fusion.39
  272.7 3.8 fusion.49
  276.8 3.8 fusion.50
  281.9 3.8 fusion.51
  285.8 2.3 fusion.41
  288.1 3.6 fusion.26
  292.6 1.6 convert_element_type.102
  295.5 1.9 fusion.18
  297.4 147.8 %all-gather.9.cloned.1.call-done = f32[2048,1024]{1,0:T(8,128)} async-done(((f32[512,1024]{1,0:T(8,128)}), f32[2048,1024]{1,0:T(8,128)}) %all-gather.9.cloned.1.call-update) | async-done | bytes 8388624 | tf_op jit(solution)/shard_map/all_gather | solution.py:235
  445.2 5.9 reduce_sum.146
  451.0 3.4 multiply_reduce_fusion
  454.5 1.3 multiply_reduce_fusion.6
  455.8 38.6 %all-reduce = (f32[1024]{0:T(1024)}, f32[128]{0:T(128)}, f32[128]{0:T(128)}, f32[1024]{0:T(1024)}) all-reduce(f32[1024]{0:T(1024)S(1)} %multiply_reduce_fusion.6, f32[128]{0:T(128)S(1)} %get-tuple-element.53, f32[128]{0:T(128)S(1)} %get-tuple-element.51, ...), channel_id=1, replica_groups=mesh['dp'=8,'tensor'=4] {'dp','tensor'}, use_global_device_ids=true, to_apply=%region_16.17 | all-reduce | flops 2304 | bytes 18432 | tf_op jit(solution)/shard_map/psum | solution.py:244
  494.4 2.3 fusion.15
  496.7 26.2 %reduce-scatter.12.cloned.1.call-done = f32[128,256]{1,0:T(8,128)} async-done(((f32[1024,256]{1,0:T(8,128)}), f32[128,256]{1,0:T(8,128)}) %reduce-scatter.12.cloned.1.call-update) | async-done | bytes 131088 | tf_op jit(solution)/shard_map/reduce_scatter | solution.py:250
  522.9 50.0 %reduce-scatter.16.cloned.1.call-done = f32[128,768]{1,0:T(8,128)} async-done(((f32[1024,768]{1,0:T(8,128)}), f32[128,768]{1,0:T(8,128)}) %reduce-scatter.16.cloned.1.call-update) | async-done | bytes 393232 | tf_op jit(solution)/shard_map/reduce_scatter | solution.py:252
  572.9 49.9 %reduce-scatter.18.cloned.1.call-done = f32[128,768]{1,0:T(8,128)} async-done(((f32[1024,768]{1,0:T(8,128)}), f32[128,768]{1,0:T(8,128)}) %reduce-scatter.18.cloned.1.call-update) | async-done | bytes 393232 | tf_op jit(solution)/shard_map/reduce_scatter | solution.py:253
  622.8 50.0 %reduce-scatter.20.cloned.1.call-done = f32[768,128]{1,0:T(8,128)} async-done(((f32[768,1024]{1,0:T(8,128)}), f32[768,128]{1,0:T(8,128)}) %reduce-scatter.20.cloned.1.call-update) | async-done | bytes 393232 | tf_op jit(solution)/shard_map/reduce_scatter | solution.py:254
  672.8 44.9 %reduce-scatter.8.cloned.1.call-done = f32[128,512]{1,0:T(8,128)} async-done(((f32[1024,512]{1,0:T(8,128)}), f32[128,512]{1,0:T(8,128)}) %reduce-scatter.8.cloned.1.call-update) | async-done | bytes 262160 | tf_op jit(solution)/shard_map/reduce_scatter | solution.py:248
  717.7 45.0 %reduce-scatter.14.cloned.1.call-done = f32[512,128]{1,0:T(8,128)} async-done(((f32[512,1024]{1,0:T(8,128)}), f32[512,128]{1,0:T(8,128)}) %reduce-scatter.14.cloned.1.call-update) | async-done | bytes 262160 | tf_op jit(solution)/shard_map/reduce_scatter | solution.py:251
  (192 shorter events, 33.1 us)
Async XLA Ops:
  7.2 139.7 %copy-start = (bf16[768,1024]{1,0:T(8,128)(2,1)S(1)}, bf16[768,1024]{1,0:T(8,128)(2,1)}, u32[]{:S(2)}) copy-start(bf16[768,1024]{1,0:T(8,128)(2,1)} %param.24) | copy-start | bytes 4718596
  7.2 35.2 %copy-start.49 = (f32[1024]{0:T(1024)S(1)}, f32[1024]{0:T(1024)}, u32[]{:S(2)}) copy-start(f32[1024]{0:T(1024)} %param.14) | copy-start | bytes 12292
  7.2 33.1 %all-gather.5.cloned.1.call-start = ((), (), s32[]{:S(2)}) async-start(), calls=%async_computation.7 | async-start | bytes 1310720 | tf_op jit(solution)/shard_map/all_gather | solution.py:136
  7.9 110.1 %all-reduce.5.cloned.1.call-start = ((), (), s32[]{:S(2)}) async-start(), calls=%async_computation.8 | async-start | bytes 2097152 | tf_op jit(solution)/shard_map/psum | solution.py:167
  9.0 33.4 %copy-start.19 = (f32[512,64]{1,0:T(8,128)}, f32[512,64]{1,0:T(8,128)S(1)}, u32[]{:S(2)}) copy-start(f32[512,64]{1,0:T(8,128)S(1)} %get-tuple-element.97) | copy-start | bytes 393220
  9.0 33.4 %copy-start.21 = (f32[512,64]{1,0:T(8,128)}, f32[512,64]{1,0:T(8,128)S(1)}, u32[]{:S(2)}) copy-start(f32[512,64]{1,0:T(8,128)S(1)} %get-tuple-element.98) | copy-start | bytes 393220
  9.2 36.8 %copy-start.34 = (f32[512,64]{0,1:T(8,128)}, f32[512,64]{0,1:T(8,128)S(1)}, u32[]{:S(2)}) copy-start(f32[512,64]{0,1:T(8,128)S(1)} %copy.27) | copy-start | bytes 393220
  42.4 19.1 %copy-start.45 = (f32[512]{0:T(512)}, f32[512]{0:T(512)S(1)}, u32[]{:S(2)}) copy-start(f32[512]{0:T(512)S(1)} %get-tuple-element.94) | copy-start | bytes 6148
  42.4 3.4 copy-start.55
  46.1 4.2 copy-start.2
  55.4 3.9 copy-start.14
  60.5 2.1 copy-start.10
  62.0 2.0 copy-start.52
  62.6 2.2 copy-start.37
  66.6 80.3 %all-gather.7.cloned.1.call-start = ((), (), s32[]{:S(2)}) async-start(), calls=%async_computation.10 | async-start | bytes 1310720 | tf_op jit(solution)/shard_map/all_gather | solution.py:177
  67.3 54.3 %copy-start.43 = (f32[1024]{0:T(1024)S(1)}, f32[1024]{0:T(1024)}, u32[]{:S(2)}) copy-start(f32[1024]{0:T(1024)} %param.21) | copy-start | bytes 12292
  67.4 174.3 %all-reduce.9.cloned.1.call-start = ((), (), s32[]{:S(2)}) async-start(), calls=%async_computation.11 | async-start | bytes 4194304 | tf_op jit(solution)/shard_map/psum | solution.py:189
  118.0 3.7 copy-start.6
  121.7 1.8 copy-start.47
  121.7 1.8 copy-start.59
  123.4 2.2 copy-start.4
  123.5 2.2 copy-start.32
  146.9 4.7 copy-start.60
  151.6 2.0 copy-start.33
  156.0 139.5 %all-reduce.7.cloned.1.call-start = ((), (), s32[]{:S(2)}) async-start(), calls=%async_computation.9 | async-start | bytes 2097152 | tf_op jit(solution)/shard_map/psum | solution.py:175
  163.8 80.4 %copy-start.7 = (bf16[512,1024]{1,0:T(8,128)(2,1)S(1)}, bf16[512,1024]{1,0:T(8,128)(2,1)}, u32[]{:S(2)}) copy-start(bf16[512,1024]{1,0:T(8,128)(2,1)} %all-reduce.5.cloned.1.call-done) | copy-start | bytes 3145732
  163.8 281.4 %all-gather.9.cloned.1.call-start = ((), (), s32[]{:S(2)}) async-start(), calls=%async_computation.19 | async-start | bytes 10485760 | tf_op jit(solution)/shard_map/all_gather | solution.py:235
  241.7 2.5 copy-start.12
  241.7 2.8 copy-start.17
  244.5 2.8 copy-start.30
  244.5 2.8 copy-start.38
  249.5 3.7 copy-start.25
  249.5 3.7 copy-start.27
  258.0 2.1 copy-start.20
  258.0 2.1 copy-start.22
  261.9 2.4 copy-start.11
  261.9 2.4 copy-start.53
  264.3 2.5 copy-start.13
  264.3 2.5 copy-start.41
  268.7 228.0 %reduce-scatter.10.cloned.1.call-start = ((), (), s32[]{:S(2)}) async-start(), calls=%async_computation.13 | async-start | bytes 1179648 | tf_op jit(solution)/shard_map/reduce_scatter | solution.py:249
  271.0 251.9 %reduce-scatter.12.cloned.1.call-start = ((), (), s32[]{:S(2)}) async-start(), calls=%async_computation.14 | async-start | bytes 1179648 | tf_op jit(solution)/shard_map/reduce_scatter | solution.py:250
  272.6 300.3 %reduce-scatter.16.cloned.1.call-start = ((), (), s32[]{:S(2)}) async-start(), calls=%async_computation.16 | async-start | bytes 3538944 | tf_op jit(solution)/shard_map/reduce_scatter | solution.py:252
  276.5 346.3 %reduce-scatter.18.cloned.1.call-start = ((), (), s32[]{:S(2)}) async-start(), calls=%async_computation.17 | async-start | bytes 3538944 | tf_op jit(solution)/shard_map/reduce_scatter | solution.py:253
  280.7 392.1 %reduce-scatter.20.cloned.1.call-start = ((), (), s32[]{:S(2)}) async-start(), calls=%async_computation.18 | async-start | bytes 3538944 | tf_op jit(solution)/shard_map/reduce_scatter | solution.py:254
  285.7 2.4 copy-start.31
  285.7 432.0 %reduce-scatter.8.cloned.1.call-start = ((), (), s32[]{:S(2)}) async-start(), calls=%async_computation.12 | async-start | bytes 2359296 | tf_op jit(solution)/shard_map/reduce_scatter | solution.py:248
  288.1 474.6 %reduce-scatter.14.cloned.1.call-start = ((), (), s32[]{:S(2)}) async-start(), calls=%async_computation.15 | async-start | bytes 2359296 | tf_op jit(solution)/shard_map/reduce_scatter | solution.py:251
  451.0 311.7 %copy-start.1 = (bf16[768,1024]{1,0:T(8,128)(2,1)S(1)}, bf16[768,1024]{1,0:T(8,128)(2,1)}, u32[]{:S(2)}) copy-start(bf16[768,1024]{1,0:T(8,128)(2,1)} %param.24) | copy-start | bytes 4718596
  (27 other events, 32.2 us)
Sparse Core Ops, SparseCore 0:
  9.6 30.6 all-gather.4
  66.7 51.2 all-reduce.4
  119.6 27.2 all-gather.6
  156.1 85.4 all-reduce.8
  243.9 50.9 all-reduce.6
  296.3 148.8 all-gather.8
  448.9 34.2 reduce-scatter.9
  486.9 35.8 reduce-scatter.11
  526.8 46.0 reduce-scatter.15
  576.7 46.0 reduce-scatter.17
  626.8 46.0 reduce-scatter.19
  676.5 41.1 reduce-scatter.7
  721.6 41.1 reduce-scatter.13
